TPU v7x, 32 devices: a whole 2x2x4 slice. The times are simulated.
32 devices in a mesh: struct: 4 (over y, x), fluid: 8 (over z, core).
Axes of the slice: x: 2, y: 2, z: 4, core: 2. Of those that a mesh axis runs over, the one named last changes fastest.
Arguments:
- shell_motion: float32 [3, 262144], P(None, ('struct', 'fluid')), may hold values from -6 to 6
- owner: int32 [262144, 1], P(('struct', 'fluid')), may hold values from 0 to 31; in each aligned block of 8192 rows (0 to 8191, 8192 to 16383, ...) at most 512 rows name the same one
- stencil_slot: int32 [4, 8, 64, 128], P(None, 'struct', 'fluid'), may hold values from 0 to 16383
- stencil_weight: float32 [4, 8, 64, 128], P(None, 'struct', 'fluid'), may hold values from 0 to 0.5
- prev_motion: float32 [3, 8, 64, 256], P(None, 'struct', 'fluid'), may hold values from -6 to 6
- node_offset: float32 [3, 8, 64, 256], P(None, 'struct', 'fluid'), may hold values from -0.07 to 0.07
- cell_split: int32 [8, 64, 256], P('struct', 'fluid'), may hold values from 0 to 3
Outputs:
- mesh_motion: float32 [3, 8, 64, 256], P(None, 'struct', 'fluid')
Inputs may be any that keep to these rules, and one draw needn't show every extreme that they name: Among the 8192 shell nodes of one device, no owner is named by more than 512 of them, a bound that some block reaches.
All inputs are finite; a program needn't handle non-finite values.
Results may differ from a plain program's by a relative error of at most 0.0003.
Values sent between devices are 32-bit elements; how exact they have to be, the bound alone decides.
A program may use at most 64 MiB of HBM per device.

v0:
```python
from functools import reduce

import jax
import jax.numpy as jnp
from jax import lax
from jax.sharding import PartitionSpec as P

SWEEPS = 4


LAMBDA_RATIO = 1.0
RELAX_FACTOR = 0.5
STEP_ORDERS = ((0, 1, 2), (0, 2, 1), (1, 0, 2), (1, 2, 0), (2, 0, 1), (2, 1, 0))
CORNER_LIST = tuple(
    ((shift_x, shift_y, shift_z) for shift_x in (0, 1) for shift_y in (0, 1) for shift_z in (0, 1))
)


def from_behind(block, axis, distance):
    devices = range(lax.axis_size(axis))
    route = [((i - distance) % len(devices), i) for i in devices]
    return lax.ppermute(block, axis, route)


def cross_product(left_vec, right_vec):
    return jnp.stack(
        [
            left_vec[1] * right_vec[2] - left_vec[2] * right_vec[1],
            left_vec[2] * right_vec[0] - left_vec[0] * right_vec[2],
            left_vec[0] * right_vec[1] - left_vec[1] * right_vec[0],
        ]
    )


def select_flip(flip_y, flip_z, unflipped, flipped_z, flipped_y, flipped_both):
    return jnp.where(
        flip_y, jnp.where(flip_z, flipped_both, flipped_y), jnp.where(flip_z, flipped_z, unflipped)
    )


def reflect_corners(corners, flip_y, flip_z):
    result = {}
    for corner in CORNER_LIST:
        shift_x, shift_y, shift_z = corner
        result[corner] = select_flip(
            flip_y,
            flip_z,
            corners[corner],
            corners[shift_x, shift_y, 1 - shift_z],
            corners[shift_x, 1 - shift_y, shift_z],
            corners[shift_x, 1 - shift_y, 1 - shift_z],
        )
    return result


def flip_masks(split_codes):
    flip_y = split_codes // 2 == 1
    flip_z = split_codes % 2 == 1
    sign_y = jnp.where(flip_y, -1.0, 1.0).astype(jnp.float32)
    sign_z = jnp.where(flip_z, -1.0, 1.0).astype(jnp.float32)
    return (flip_y, flip_z, sign_y, sign_z)


def lattice_edge(vertex, sign_y, sign_z):
    return jnp.stack(
        [jnp.full_like(sign_y, float(vertex[0])), sign_y * vertex[1], sign_z * vertex[2]]
    )


def element_gradients(offsets, step_order, sign_y, sign_z):
    position = [0, 0, 0]
    vertex_path = [(0, 0, 0)]
    for axis_id in step_order:
        position[axis_id] = 1
        vertex_path.append(tuple(position))
    anchor = offsets[vertex_path[0]]
    edge_list = [
        lattice_edge(vertex, sign_y, sign_z) + offsets[vertex] - anchor
        for vertex in vertex_path[1:]
    ]
    across_one = cross_product(edge_list[1], edge_list[2])
    across_two = cross_product(edge_list[2], edge_list[0])
    across_three = cross_product(edge_list[0], edge_list[1])
    volume_six = jnp.sum(edge_list[0] * across_one, axis=0)
    grad_one = across_one / volume_six
    grad_two = across_two / volume_six
    grad_three = across_three / volume_six
    grad_zero = -(grad_one + grad_two + grad_three)
    return (vertex_path, [grad_zero, grad_one, grad_two, grad_three])


def element_forces(offsets, displace, sign_y, sign_z):
    forces = {corner: jnp.zeros_like(displace[corner]) for corner in CORNER_LIST}
    for step_order in STEP_ORDERS:
        vertex_path, gradient_list = element_gradients(offsets, step_order, sign_y, sign_z)
        tensor = displace[vertex_path[0]][:, None] * gradient_list[0][None, :]
        for vertex in range(1, 4):
            tensor = (
                tensor + displace[vertex_path[vertex]][:, None] * gradient_list[vertex][None, :]
            )
        trace_sum = tensor[0, 0] + tensor[1, 1] + tensor[2, 2]
        symmetric = tensor + jnp.swapaxes(tensor, 0, 1)
        for vertex in range(4):
            gradient = gradient_list[vertex]
            nodal_force = LAMBDA_RATIO * trace_sum * gradient + jnp.sum(
                symmetric * gradient[None, :], axis=1
            )
            forces[vertex_path[vertex]] = forces[vertex_path[vertex]] + nodal_force
    return forces


def element_diagonal(offsets, sign_y, sign_z):
    result = {corner: jnp.zeros_like(offsets[corner]) for corner in CORNER_LIST}
    for step_order in STEP_ORDERS:
        vertex_path, gradient_list = element_gradients(offsets, step_order, sign_y, sign_z)
        for vertex in range(4):
            gradient = gradient_list[vertex]
            entry = (LAMBDA_RATIO + 1.0) * gradient * gradient + jnp.sum(
                gradient * gradient, axis=0
            )
            result[vertex_path[vertex]] = result[vertex_path[vertex]] + entry
    return result


def cell_corners(extended, count_y, count_z):
    return {
        corner: jnp.roll(
            extended[:, corner[1] : corner[1] + count_y, corner[2] : corner[2] + count_z, :],
            -corner[0],
            axis=3,
        )
        for corner in CORNER_LIST
    }


def corner_diagonal(offset_ext, masks, count_y, count_z):
    flip_y, flip_z, sign_y, sign_z = masks
    offsets = reflect_corners(cell_corners(offset_ext, count_y, count_z), flip_y, flip_z)
    return reflect_corners(element_diagonal(offsets, sign_y, sign_z), flip_y, flip_z)


def corner_forces(offset_ext, motion_ext, masks, count_y, count_z):
    flip_y, flip_z, sign_y, sign_z = masks
    offsets = reflect_corners(cell_corners(offset_ext, count_y, count_z), flip_y, flip_z)
    displace = reflect_corners(cell_corners(motion_ext, count_y, count_z), flip_y, flip_z)
    return reflect_corners(element_forces(offsets, displace, sign_y, sign_z), flip_y, flip_z)


def spread_sum(per_corner):
    pieces = [
        jnp.roll(
            jnp.pad(
                per_corner[corner],
                ((0, 0), (corner[1], 1 - corner[1]), (corner[2], 1 - corner[2]), (0, 0)),
            ),
            corner[0],
            axis=3,
        )
        for corner in CORNER_LIST
    ]
    return reduce(jnp.add, pieces)


def upper_ghosts(nodal_field):
    top_plane = from_behind(nodal_field[:, :, :1, :], "fluid", -1)
    widened = jnp.concatenate([nodal_field, top_plane], axis=2)
    row_part = from_behind(widened[:, :1], "struct", -1)
    return jnp.concatenate([widened, row_part], axis=1)


def fold_back(spread):
    count_y = spread.shape[1] - 1
    count_z = spread.shape[2] - 1
    row_part = from_behind(spread[:, count_y:], "struct", 1)
    folded = jnp.concatenate([spread[:, :1] + row_part, spread[:, 1:count_y]], axis=1)
    top_plane = from_behind(folded[:, :, count_z:], "fluid", 1)
    return jnp.concatenate([folded[:, :, :1] + top_plane, folded[:, :, 1:count_z]], axis=2)


def shards(shell_motion, owner, stencil_slot, stencil_weight, prev_motion, node_offset, cell_split):
    struct_count = lax.axis_size("struct")
    fluid_count = lax.axis_size("fluid")
    devices = struct_count * fluid_count
    capacity = 2 * shell_motion.shape[1] // devices
    targets = jnp.arange(devices, dtype=jnp.int32)
    owner_rows = owner[:, 0]
    onehot = (owner_rows[:, None] == targets[None, :]).astype(jnp.int32)
    before = jnp.cumsum(onehot, axis=0) - onehot
    slot_rank = jnp.sum(before * onehot, axis=1)
    slot_place = owner_rows * capacity + slot_rank
    packed = jnp.zeros((3, devices * capacity), jnp.float32).at[:, slot_place].set(shell_motion)
    received = lax.all_to_all(
        packed.reshape(3, devices, capacity),
        ("struct", "fluid"),
        split_axis=1,
        concat_axis=1,
        tiled=True,
    )
    received = received.reshape(3, devices * capacity)
    stencil_count, count_y, count_z, wall_width = stencil_slot.shape
    gathered = jnp.take(received, stencil_slot.reshape(-1), axis=1).reshape(
        3, stencil_count, count_y, count_z, wall_width
    )
    wall_values = jnp.sum(stencil_weight[None] * gathered, axis=1)
    motion = jnp.concatenate([wall_values, prev_motion[:, :, :, wall_width:]], axis=3)
    is_wall = (jnp.arange(motion.shape[3], dtype=jnp.int32) < wall_width)[None, None, None, :]
    masks = flip_masks(cell_split)
    offset_ext = upper_ghosts(node_offset)
    diagonal = fold_back(spread_sum(corner_diagonal(offset_ext, masks, count_y, count_z)))
    for sweep_index in range(SWEEPS):
        forces = fold_back(
            spread_sum(corner_forces(offset_ext, upper_ghosts(motion), masks, count_y, count_z))
        )
        motion = jnp.where(is_wall, motion, motion - RELAX_FACTOR * forces / diagonal)
    return motion


def solution(mesh):
    return jax.shard_map(
        shards,
        mesh=mesh,
        in_specs=(
            P(None, ("struct", "fluid")),
            P(("struct", "fluid"), None),
            P(None, "struct", "fluid", None),
            P(None, "struct", "fluid", None),
            P(None, "struct", "fluid", None),
            P(None, "struct", "fluid", None),
            P("struct", "fluid", None),
        ),
        out_specs=P(None, "struct", "fluid", None),
        check_vma=False,
    )
```

profile of v0, /device:TPU:0, one launch (start us, length us, event | category | flops | bytes accessed | tf_op | source)
XLA Modules:
  0.0 182.4 jit_solution(8208545161125621086)
XLA Ops:
  0.8 4.5 %collective-permute-start.2 = (f32[3,2,1,256]{3,2,1,0:T(1,128)S(1)}, f32[3,2,1,256]{3,2,1,0:T(1,128)S(1)}, u32[]{:S(2)}, u32[]{:S(2)}) collective-permute-start(f32[3,2,1,256]{3,2,1,0:T(1,128)S(1)} %slice.619), channel_id=1, source_target_pairs={{1,0},{2,1},{3,2},{4,3},{5,4},{6,5},{7,6},{0,7},{9,8},{10,9},{11,1... | collective-permute-start | bytes 18440 | tf_op jit(solution)/shard_map/ppermute | solution.py:22
  6.2 9.5 %reduce-window.6 = s32[32,64,128]{2,1,0:T(8,128)S(1)} reduce-window(s32[32,64,128]{2,1,0:T(8,128)S(1)} %fusion.5, s32[]{:T(128)} %constant.36.clone.1), window={size=1x1x128 pad=0_0x0_0x127_0}, to_apply=%region_0.0 | reduce-window | flops 33292288 | bytes 2097156 | tf_op jit(solution)/shard_map/reduce-window
  18.1 2.7 %copy.1340 = f32[8192,3]{1,0:T(8,128)} copy(f32[8192,3]{0,1:T(4,128)S(1)} %bitcast.96) | data formatting | bytes 196608 | tf_op args[0]
  20.8 24.5 %scatter_custom_fusion = f32[3,16384]{0,1:T(8,128)} fusion(s32[8192]{0:T(1024)S(1)} %bitcast.101, f32[8192,3]{1,0:T(8,128)} %copy.1340, f32[]{:T(128)} %constant.58.clone.1), kind=kCustom, calls=%fused_computation.3 | custom fusion | bytes 197120 | tf_op jit(solution)/shard_map/scatter | solution.py:191
  45.3 6.0 %copy.1341 = f32[3,32,512]{2,0,1:T(4,128)} copy(f32[3,32,512]{0,2,1:T(8,128)} %bitcast.89) | data formatting | bytes 393216 | tf_op jit(solution)/shard_map/reshape | solution.py:193
  51.3 2.9 %all-to-all-start = ((f32[3,32,512]{2,0,1:T(4,128)}), f32[3,32,512]{2,0,1:T(4,128)S(1)}, u32[]{:S(2)}, u32[]{:S(2)}) async-start(f32[3,32,512]{2,0,1:T(4,128)} %copy.1341), calls=%async_computation | async-start | bytes 524288 | tf_op jit(solution)/shard_map/all_to_all | solution.py:192
  54.5 2.7 %collective-permute-start.3 = (f32[3,1,9,256]{3,1,2,0:T(1,128)S(1)}, f32[3,1,9,256]{3,1,2,0:T(1,128)S(1)}, u32[]{:S(2)}, u32[]{:S(2)}) collective-permute-start(f32[3,1,9,256]{3,1,2,0:T(1,128)S(1)} %copy.1346), channel_id=1, source_target_pairs={{8,0},{16,8},{24,16},{0,24},{9,1},{17,9},{25,17},{1,25},{10,2},{18... | collective-permute-start | bytes 82952 | tf_op jit(solution)/shard_map/ppermute | solution.py:22
  59.3 4.9 %all-to-all-done = f32[3,32,512]{2,0,1:T(4,128)S(1)} async-done(((f32[3,32,512]{2,0,1:T(4,128)}), f32[3,32,512]{2,0,1:T(4,128)S(1)}, u32[]{:S(2)}, u32[]{:S(2)}) %all-to-all-start) | async-done | bytes 196640 | tf_op jit(solution)/shard_map/all_to_all | solution.py:192
  64.2 4.8 %copy.1342 = f32[3,32,512]{0,2,1:T(8,128)} copy(f32[3,32,512]{2,0,1:T(4,128)S(1)} %all-to-all-done) | data formatting | bytes 393216 | tf_op jit(solution)/shard_map/all_to_all | solution.py:192
  69.0 31.1 %gather_fusion = f32[8192,3]{1,0:T(8,128)} fusion(f32[3,16384]{0,1:T(8,128)} %bitcast.90, s32[8192]{0:T(1024)S(1)} %broadcast_clamp_fusion), kind=kCustom, calls=%fused_computation | custom fusion | bytes 229376 | tf_op jit(solution)/shard_map/jit(_take)/gather | solution.py:201
  100.1 6.1 %multiply_reduce_fusion = f32[3,2,8,128]{0,3,2,1:T(8,128)S(1)} fusion(f32[3,4,2,8,128]{0,4,3,2,1:T(8,128)} %bitcast.91, f32[4,2,8,128]{3,2,1,0:T(8,128)S(1)} %copy-done.4, pred[4,2,8,128]{3,2,1,0:T(8,128)(4,1)S(1)} %compare_and_fusion), kind=kLoop, calls=%fused_computation.2 | loop fusion | flops 67584 | bytes 163840 | tf_op jit(solution)/shard_map/reduce_sum | solution.py:204
  110.8 3.0 %collective-permute-done.1 = f32[3,1,9,256]{3,1,2,0:T(1,128)S(1)} collective-permute-done((f32[3,1,9,256]{3,1,2,0:T(1,128)S(1)}, f32[3,1,9,256]{3,1,2,0:T(1,128)S(1)}, u32[]{:S(2)}, u32[]{:S(2)}) %collective-permute-start.1) | collective-permute-done | bytes 27680 | tf_op jit(solution)/shard_map/ppermute | solution.py:22
  119.8 2.4 %collective-permute-done.6 = f32[3,1,9,256]{3,1,2,0:T(1,128)S(1)} collective-permute-done((f32[3,1,9,256]{3,1,2,0:T(1,128)S(1)}, f32[3,1,9,256]{3,1,2,0:T(1,128)S(1)}, u32[]{:S(2)}, u32[]{:S(2)}) %collective-permute-start.6) | collective-permute-done | bytes 27680 | tf_op jit(solution)/shard_map/ppermute | solution.py:22
  124.7 2.6 %collective-permute-done.7 = f32[3,2,1,256]{3,1,2,0:T(2,128)S(1)} collective-permute-done((f32[3,2,1,256]{3,1,2,0:T(2,128)S(1)}, f32[3,2,1,256]{3,1,2,0:T(2,128)S(1)}, u32[]{:S(2)}, u32[]{:S(2)}) %collective-permute-start.7) | collective-permute-done | bytes 6176 | tf_op jit(solution)/shard_map/ppermute | solution.py:22
  127.3 2.2 %collective-permute-done.5 = f32[3,2,1,256]{3,1,2,0:T(2,128)S(1)} collective-permute-done((f32[3,2,1,256]{3,1,2,0:T(2,128)S(1)}, f32[3,2,1,256]{3,1,2,0:T(2,128)S(1)}, u32[]{:S(2)}, u32[]{:S(2)}) %collective-permute-start.5) | collective-permute-done | bytes 6176 | tf_op jit(solution)/shard_map/ppermute | solution.py:22
  131.5 3.4 %collective-permute-done.9 = f32[3,1,9,256]{3,1,2,0:T(1,128)S(1)} collective-permute-done((f32[3,1,9,256]{3,1,2,0:T(1,128)S(1)}, f32[3,1,9,256]{3,1,2,0:T(1,128)S(1)}, u32[]{:S(2)}, u32[]{:S(2)}) %collective-permute-start.9) | collective-permute-done | bytes 27680 | tf_op jit(solution)/shard_map/ppermute | solution.py:22
  137.4 4.5 %collective-permute-done.10 = f32[3,1,9,256]{3,1,2,0:T(1,128)S(1)} collective-permute-done((f32[3,1,9,256]{3,1,2,0:T(1,128)S(1)}, f32[3,1,9,256]{3,1,2,0:T(1,128)S(1)}, u32[]{:S(2)}, u32[]{:S(2)}) %collective-permute-start.10) | collective-permute-done | bytes 27680 | tf_op jit(solution)/shard_map/ppermute | solution.py:22
  142.2 4.8 %collective-permute-done.11 = f32[3,2,1,256]{3,1,2,0:T(2,128)S(1)} collective-permute-done((f32[3,2,1,256]{3,1,2,0:T(2,128)S(1)}, f32[3,2,1,256]{3,1,2,0:T(2,128)S(1)}, u32[]{:S(2)}, u32[]{:S(2)}) %collective-permute-start.11) | collective-permute-done | bytes 6176 | tf_op jit(solution)/shard_map/ppermute | solution.py:22
  148.9 3.4 %collective-permute-done.13 = f32[3,1,9,256]{3,1,2,0:T(1,128)S(1)} collective-permute-done((f32[3,1,9,256]{3,1,2,0:T(1,128)S(1)}, f32[3,1,9,256]{3,1,2,0:T(1,128)S(1)}, u32[]{:S(2)}, u32[]{:S(2)}) %collective-permute-start.13) | collective-permute-done | bytes 27680 | tf_op jit(solution)/shard_map/ppermute | solution.py:22
  154.8 4.5 %collective-permute-done.14 = f32[3,1,9,256]{3,1,2,0:T(1,128)S(1)} collective-permute-done((f32[3,1,9,256]{3,1,2,0:T(1,128)S(1)}, f32[3,1,9,256]{3,1,2,0:T(1,128)S(1)}, u32[]{:S(2)}, u32[]{:S(2)}) %collective-permute-start.14) | collective-permute-done | bytes 27680 | tf_op jit(solution)/shard_map/ppermute | solution.py:22
  159.6 4.8 %collective-permute-done.15 = f32[3,2,1,256]{3,1,2,0:T(2,128)S(1)} collective-permute-done((f32[3,2,1,256]{3,1,2,0:T(2,128)S(1)}, f32[3,2,1,256]{3,1,2,0:T(2,128)S(1)}, u32[]{:S(2)}, u32[]{:S(2)}) %collective-permute-start.15) | collective-permute-done | bytes 6176 | tf_op jit(solution)/shard_map/ppermute | solution.py:22
  166.3 3.4 %collective-permute-done.17 = f32[3,1,9,256]{3,1,2,0:T(1,128)S(1)} collective-permute-done((f32[3,1,9,256]{3,1,2,0:T(1,128)S(1)}, f32[3,1,9,256]{3,1,2,0:T(1,128)S(1)}, u32[]{:S(2)}, u32[]{:S(2)}) %collective-permute-start.17) | collective-permute-done | bytes 27680 | tf_op jit(solution)/shard_map/ppermute | solution.py:22
  172.2 4.5 %collective-permute-done.18 = f32[3,1,9,256]{3,1,2,0:T(1,128)S(1)} collective-permute-done((f32[3,1,9,256]{3,1,2,0:T(1,128)S(1)}, f32[3,1,9,256]{3,1,2,0:T(1,128)S(1)}, u32[]{:S(2)}, u32[]{:S(2)}) %collective-permute-start.18) | collective-permute-done | bytes 27680 | tf_op jit(solution)/shard_map/ppermute | solution.py:22
  177.0 4.8 %collective-permute-done.19 = f32[3,2,1,256]{3,1,2,0:T(2,128)S(1)} collective-permute-done((f32[3,2,1,256]{3,1,2,0:T(2,128)S(1)}, f32[3,2,1,256]{3,1,2,0:T(2,128)S(1)}, u32[]{:S(2)}, u32[]{:S(2)}) %collective-permute-start.19) | collective-permute-done | bytes 6176 | tf_op jit(solution)/shard_map/ppermute | solution.py:22
  (327 shorter events, 32.5 us)
Async XLA Ops:
  0.0 17.2 %copy-start.1 = (s32[8192,1]{0,1:T(1,128)S(1)}, s32[8192,1]{0,1:T(1,128)}, u32[]{:S(2)}) copy-start(s32[8192,1]{0,1:T(1,128)} %param.8) | copy-start | bytes 98308
  0.0 18.1 %copy-start.2 = (f32[3,8192]{1,0:T(4,128)S(1)}, f32[3,8192]{1,0:T(4,128)}, u32[]{:S(2)}) copy-start(f32[3,8192]{1,0:T(4,128)} %param.7) | copy-start | bytes 294916
  0.8 53.5 %collective-permute-start.2 = (f32[3,2,1,256]{3,2,1,0:T(1,128)S(1)}, f32[3,2,1,256]{3,2,1,0:T(1,128)S(1)}, u32[]{:S(2)}, u32[]{:S(2)}) collective-permute-start(f32[3,2,1,256]{3,2,1,0:T(1,128)S(1)} %slice.619), channel_id=1, source_target_pairs={{1,0},{2,1},{3,2},{4,3},{5,4},{6,5},{7,6},{0,7},{9,8},{10,9},{11,1... | collective-permute-start | bytes 18440 | tf_op jit(solution)/shard_map/ppermute | solution.py:22
  51.3 12.9 %all-to-all-start = ((f32[3,32,512]{2,0,1:T(4,128)}), f32[3,32,512]{2,0,1:T(4,128)S(1)}, u32[]{:S(2)}, u32[]{:S(2)}) async-start(f32[3,32,512]{2,0,1:T(4,128)} %copy.1341), calls=%async_computation | async-start | bytes 524288 | tf_op jit(solution)/shard_map/all_to_all | solution.py:192
  54.5 4.3 %collective-permute-start.3 = (f32[3,1,9,256]{3,1,2,0:T(1,128)S(1)}, f32[3,1,9,256]{3,1,2,0:T(1,128)S(1)}, u32[]{:S(2)}, u32[]{:S(2)}) collective-permute-start(f32[3,1,9,256]{3,1,2,0:T(1,128)S(1)} %copy.1346), channel_id=1, source_target_pairs={{8,0},{16,8},{24,16},{0,24},{9,1},{17,9},{25,17},{1,25},{10,2},{18... | collective-permute-start | bytes 82952 | tf_op jit(solution)/shard_map/ppermute | solution.py:22
  59.3 40.8 %copy-start.4 = (f32[4,2,8,128]{3,2,1,0:T(8,128)S(1)}, f32[4,2,8,128]{3,2,1,0:T(8,128)}, u32[]{:S(2)}) copy-start(f32[4,2,8,128]{3,2,1,0:T(8,128)} %param.10) | copy-start | bytes 98308
  106.6 3.0 %collective-permute-start = (f32[3,2,1,256]{3,2,1,0:T(1,128)S(1)}, f32[3,2,1,256]{3,2,1,0:T(1,128)S(1)}, u32[]{:S(2)}, u32[]{:S(2)}) collective-permute-start(f32[3,2,1,256]{3,2,1,0:T(1,128)S(1)} %fusion.198), channel_id=1, source_target_pairs={{1,0},{2,1},{3,2},{4,3},{5,4},{6,5},{7,6},{0,7},{9,8},{10,9},{11,1... | collective-permute-start | bytes 18440 | tf_op jit(solution)/shard_map/ppermute | solution.py:22
  109.7 4.1 %collective-permute-start.1 = (f32[3,1,9,256]{3,1,2,0:T(1,128)S(1)}, f32[3,1,9,256]{3,1,2,0:T(1,128)S(1)}, u32[]{:S(2)}, u32[]{:S(2)}) collective-permute-start(f32[3,1,9,256]{3,1,2,0:T(1,128)S(1)} %copy.1344), channel_id=1, source_target_pairs={{8,0},{16,8},{24,16},{0,24},{9,1},{17,9},{25,17},{1,25},{10,2},{18... | collective-permute-start | bytes 82952 | tf_op jit(solution)/shard_map/ppermute | solution.py:22
  117.4 4.8 %collective-permute-start.6 = (f32[3,1,9,256]{3,1,2,0:T(1,128)S(1)}, f32[3,1,9,256]{3,1,2,0:T(1,128)S(1)}, u32[]{:S(2)}, u32[]{:S(2)}) collective-permute-start(f32[3,1,9,256]{3,1,2,0:T(1,128)S(1)} %copy.1355), channel_id=1, source_target_pairs={{24,0},{0,8},{8,16},{16,24},{25,1},{1,9},{9,17},{17,25},{26,2},{2,... | collective-permute-start | bytes 82952 | tf_op jit(solution)/shard_map/ppermute | solution.py:22
  119.4 4.8 %collective-permute-start.4 = (f32[3,1,9,256]{3,1,2,0:T(1,128)S(1)}, f32[3,1,9,256]{3,1,2,0:T(1,128)S(1)}, u32[]{:S(2)}, u32[]{:S(2)}) collective-permute-start(f32[3,1,9,256]{3,1,2,0:T(1,128)S(1)} %copy.1349), channel_id=1, source_target_pairs={{24,0},{0,8},{8,16},{16,24},{25,1},{1,9},{9,17},{17,25},{26,2},{2,... | collective-permute-start | bytes 82952 | tf_op jit(solution)/shard_map/ppermute | solution.py:22
  122.3 4.9 %collective-permute-start.7 = (f32[3,2,1,256]{3,1,2,0:T(2,128)S(1)}, f32[3,2,1,256]{3,1,2,0:T(2,128)S(1)}, u32[]{:S(2)}, u32[]{:S(2)}) collective-permute-start(f32[3,2,1,256]{3,1,2,0:T(2,128)S(1)} %pad_maximum_fusion.52), channel_id=1, source_target_pairs={{7,0},{0,1},{1,2},{2,3},{3,4},{4,5},{5,6},{6,7},{15,8},{8,9},{9,10... | collective-permute-start | bytes 18440 | tf_op jit(solution)/shard_map/ppermute | solution.py:22
  124.4 5.1 %collective-permute-start.5 = (f32[3,2,1,256]{3,1,2,0:T(2,128)S(1)}, f32[3,2,1,256]{3,1,2,0:T(2,128)S(1)}, u32[]{:S(2)}, u32[]{:S(2)}) collective-permute-start(f32[3,2,1,256]{3,1,2,0:T(2,128)S(1)} %pad_maximum_fusion.53), channel_id=1, source_target_pairs={{7,0},{0,1},{1,2},{2,3},{3,4},{4,5},{5,6},{6,7},{15,8},{8,9},{9,10... | collective-permute-start | bytes 18440 | tf_op jit(solution)/shard_map/ppermute | solution.py:22
  129.6 1.4 collective-permute-start.8
  131.0 3.9 %collective-permute-start.9 = (f32[3,1,9,256]{3,1,2,0:T(1,128)S(1)}, f32[3,1,9,256]{3,1,2,0:T(1,128)S(1)}, u32[]{:S(2)}, u32[]{:S(2)}) collective-permute-start(f32[3,1,9,256]{3,1,2,0:T(1,128)S(1)} %copy.1361), channel_id=1, source_target_pairs={{8,0},{16,8},{24,16},{0,24},{9,1},{17,9},{25,17},{1,25},{10,2},{18... | collective-permute-start | bytes 82952 | tf_op jit(solution)/shard_map/ppermute | solution.py:22
  137.1 4.8 %collective-permute-start.10 = (f32[3,1,9,256]{3,1,2,0:T(1,128)S(1)}, f32[3,1,9,256]{3,1,2,0:T(1,128)S(1)}, u32[]{:S(2)}, u32[]{:S(2)}) collective-permute-start(f32[3,1,9,256]{3,1,2,0:T(1,128)S(1)} %copy.1363), channel_id=1, source_target_pairs={{24,0},{0,8},{8,16},{16,24},{25,1},{1,9},{9,17},{17,25},{26,2},{2,... | collective-permute-start | bytes 82952 | tf_op jit(solution)/shard_map/ppermute | solution.py:22
  142.0 4.9 %collective-permute-start.11 = (f32[3,2,1,256]{3,1,2,0:T(2,128)S(1)}, f32[3,2,1,256]{3,1,2,0:T(2,128)S(1)}, u32[]{:S(2)}, u32[]{:S(2)}) collective-permute-start(f32[3,2,1,256]{3,1,2,0:T(2,128)S(1)} %pad_maximum_fusion.51), channel_id=1, source_target_pairs={{7,0},{0,1},{1,2},{2,3},{3,4},{4,5},{5,6},{6,7},{15,8},{8,9},{9,10... | collective-permute-start | bytes 18440 | tf_op jit(solution)/shard_map/ppermute | solution.py:22
  147.0 1.4 collective-permute-start.12
  148.5 3.9 %collective-permute-start.13 = (f32[3,1,9,256]{3,1,2,0:T(1,128)S(1)}, f32[3,1,9,256]{3,1,2,0:T(1,128)S(1)}, u32[]{:S(2)}, u32[]{:S(2)}) collective-permute-start(f32[3,1,9,256]{3,1,2,0:T(1,128)S(1)} %copy.1369), channel_id=1, source_target_pairs={{8,0},{16,8},{24,16},{0,24},{9,1},{17,9},{25,17},{1,25},{10,2},{18... | collective-permute-start | bytes 82952 | tf_op jit(solution)/shard_map/ppermute | solution.py:22
  154.5 4.8 %collective-permute-start.14 = (f32[3,1,9,256]{3,1,2,0:T(1,128)S(1)}, f32[3,1,9,256]{3,1,2,0:T(1,128)S(1)}, u32[]{:S(2)}, u32[]{:S(2)}) collective-permute-start(f32[3,1,9,256]{3,1,2,0:T(1,128)S(1)} %copy.1371), channel_id=1, source_target_pairs={{24,0},{0,8},{8,16},{16,24},{25,1},{1,9},{9,17},{17,25},{26,2},{2,... | collective-permute-start | bytes 82952 | tf_op jit(solution)/shard_map/ppermute | solution.py:22
  159.4 4.9 %collective-permute-start.15 = (f32[3,2,1,256]{3,1,2,0:T(2,128)S(1)}, f32[3,2,1,256]{3,1,2,0:T(2,128)S(1)}, u32[]{:S(2)}, u32[]{:S(2)}) collective-permute-start(f32[3,2,1,256]{3,1,2,0:T(2,128)S(1)} %pad_maximum_fusion.50), channel_id=1, source_target_pairs={{7,0},{0,1},{1,2},{2,3},{3,4},{4,5},{5,6},{6,7},{15,8},{8,9},{9,10... | collective-permute-start | bytes 18440 | tf_op jit(solution)/shard_map/ppermute | solution.py:22
  164.4 1.4 collective-permute-start.16
  165.9 3.9 %collective-permute-start.17 = (f32[3,1,9,256]{3,1,2,0:T(1,128)S(1)}, f32[3,1,9,256]{3,1,2,0:T(1,128)S(1)}, u32[]{:S(2)}, u32[]{:S(2)}) collective-permute-start(f32[3,1,9,256]{3,1,2,0:T(1,128)S(1)} %copy.1377), channel_id=1, source_target_pairs={{8,0},{16,8},{24,16},{0,24},{9,1},{17,9},{25,17},{1,25},{10,2},{18... | collective-permute-start | bytes 82952 | tf_op jit(solution)/shard_map/ppermute | solution.py:22
  171.9 4.8 %collective-permute-start.18 = (f32[3,1,9,256]{3,1,2,0:T(1,128)S(1)}, f32[3,1,9,256]{3,1,2,0:T(1,128)S(1)}, u32[]{:S(2)}, u32[]{:S(2)}) collective-permute-start(f32[3,1,9,256]{3,1,2,0:T(1,128)S(1)} %copy.1379), channel_id=1, source_target_pairs={{24,0},{0,8},{8,16},{16,24},{25,1},{1,9},{9,17},{17,25},{26,2},{2,... | collective-permute-start | bytes 82952 | tf_op jit(solution)/shard_map/ppermute | solution.py:22
  176.8 4.9 %collective-permute-start.19 = (f32[3,2,1,256]{3,1,2,0:T(2,128)S(1)}, f32[3,2,1,256]{3,1,2,0:T(2,128)S(1)}, u32[]{:S(2)}, u32[]{:S(2)}) collective-permute-start(f32[3,2,1,256]{3,1,2,0:T(2,128)S(1)} %pad_maximum_fusion.49), channel_id=1, source_target_pairs={{7,0},{0,1},{1,2},{2,3},{3,4},{4,5},{5,6},{6,7},{15,8},{8,9},{9,10... | collective-permute-start | bytes 18440 | tf_op jit(solution)/shard_map/ppermute | solution.py:22
  (4 other events, 38.9 us)
where the time goes:
time: 183 us; the launch traced here: 182 us
  local copies, waits for them, and re-layouts  74.3 us (41%)
  waiting for transfers between devices  61.8 us (34%)
  other arithmetic  27 us (15%)
  starting transfers between devices  17.5 us (10%)
  between operations  1.87 us (1%)
    ppermute x20, waiting for transfers between devices, from_behind(): return lax.ppermute(block, axis, route)  56.9 us
    gather x1, local copies, waits for them, and re-layouts, shards(): jnp.take(received, stencil_slot.reshape(-1), axis=1)  31.1 us
    scatter x1, local copies, waits for them, and re-layouts, shards(): jnp.zeros((3, devices * capacity), jnp.float32).at[:, slot_place]  24.5 us
    ppermute x20, starting transfers between devices, from_behind(): return lax.ppermute(block, axis, route)  14.6 us
    another operation x3, other arithmetic  10.1 us
    reduce_sum x1, other arithmetic, shards(): wall_values = jnp.sum(stencil_weight[None] * gathered, axis=1)  6.13 us
    reshape x1, local copies, waits for them, and re-layouts, shards(): packed.reshape(3, devices, capacity)  5.95 us
    all_to_all x1, waiting for transfers between devices, shards(): lax.all_to_all(packed.reshape(3, devices, capacity), ('struct', 'fluid'),...  4.88 us
  transfers between devices with their start and end apart: 21, of which 20 were waited for; matrix products, arithmetic and copies ran while one was open for 26% of the time, Pallas kernels for 0%

commit v1 on v0

v1 whole, which is shorter than its diff:
```python
import functools

import jax
import jax.numpy as jnp
from jax import lax
from jax.experimental import pallas as pl
from jax.experimental.pallas import tpu as pltpu
from jax.sharding import PartitionSpec as P

SWEEPS = 4
LANES = 128
LAMBDA_RATIO = 1.0
RELAX_FACTOR = 0.5
STEP_ORDERS = ((0, 1, 2), (0, 2, 1), (1, 0, 2), (1, 2, 0), (2, 0, 1), (2, 1, 0))
CORNERS = tuple((a, b, c) for a in (0, 1) for b in (0, 1) for c in (0, 1))
BF16 = jnp.bfloat16
F32 = jnp.float32


def from_behind(block, axis, distance):
    count = lax.axis_size(axis)
    route = [((i - distance) % count, i) for i in range(count)]
    return lax.ppermute(block, axis, route)


def widen(block, axis, dim, depth):
    count, size = lax.axis_size(axis), block.shape[dim]
    whole = {0: block}

    def part(distance, low, high):
        key = distance % count
        if high - low < size and key != 0:
            return from_behind(lax.slice_in_dim(block, low, high, axis=dim), axis, distance)
        if key not in whole:
            whole[key] = from_behind(block, axis, distance)
        return lax.slice_in_dim(whole[key], low, high, axis=dim)

    below, above, left = [], [], depth
    distance = 1
    while left > 0:
        taken = min(left, size)
        below.insert(0, part(distance, size - taken, size))
        above.append(part(-distance, 0, taken))
        left -= taken
        distance += 1
    return jnp.concatenate(below + [block] + above, axis=dim)


def split_two(values):
    high = values.astype(BF16)
    low = (values - high.astype(F32)).astype(BF16)
    return high, low


def iota(shape, dim):
    return lax.broadcasted_iota(jnp.int32, shape, dim)


def pack_kernel(devices, capacity, own_ref, val_ref, out_ref, place_ref, acc_ref):
    rows = own_ref.shape[0]
    wide = 2 * LANES
    groups = devices * capacity // wide
    own = own_ref[...]
    upper = (iota((LANES, LANES), 0) < iota((LANES, LANES), 1)).astype(F32)
    prefix_all = jnp.concatenate([upper, jnp.ones((LANES, LANES), F32)], axis=1).astype(BF16)
    lower = (iota((rows, rows), 1) < iota((rows, rows), 0)).astype(F32).astype(BF16)
    chunk = min(devices, 32)

    def ranks(step, place):
        for o in range(chunk):
            target = step * chunk + o
            named = own == target
            both = jnp.dot(named.astype(F32).astype(BF16), prefix_all, preferred_element_type=F32)
            ahead = jnp.dot(lower, both[:, LANES:].astype(BF16), preferred_element_type=F32)
            rank = (both[:, :LANES] + ahead).astype(jnp.int32)
            place = jnp.where(named, rank + target * capacity, place)
        return place

    place = jnp.zeros((rows, LANES), jnp.int32)
    if chunk == devices:
        place = ranks(0, place)
    else:
        place = lax.fori_loop(0, devices // chunk, ranks, place)
    place_ref[...] = place
    acc_ref[...] = jnp.zeros_like(acc_ref)
    group_id = iota((groups, LANES), 0)
    lane_id = iota((wide, LANES), 0)

    def spread(step, carry):
        total = None
        for u in range(4):
            row = step * 4 + u
            at = place_ref[pl.ds(row, 1), :]
            hit = group_id == at // wide
            column = (lane_id == at % wide).astype(F32).astype(BF16)
            parts = []
            for c in range(3):
                value = val_ref[c, pl.ds(row, 1), :]
                high = value.astype(BF16).astype(F32)
                low = value - high
                parts.append(
                    jnp.concatenate(
                        [jnp.where(hit, high, 0.0).astype(BF16), jnp.where(hit, low, 0.0).astype(BF16)],
                        axis=1,
                    )
                )
            left = jnp.concatenate(parts, axis=0)
            right = jnp.concatenate([column, column], axis=1)
            product = lax.dot_general(
                left, right, (((1,), (1,)), ((), ())), preferred_element_type=F32
            )
            total = product if total is None else total + product
        acc_ref[...] += total
        return carry

    lax.fori_loop(0, rows // 4, spread, 0)
    pieces = capacity // LANES
    for o in range(devices):
        for c in range(3):
            for b in range(pieces):
                m = o * pieces + b
                out_ref[o, pl.ds(c * pieces + b, 1), :] = acc_ref[
                    pl.ds(c * groups + m // 2, 1), pl.ds((m % 2) * LANES, LANES)
                ]


def wall_kernel(recv_ref, slot_ref, weight_ref, out_ref, table_ref, both_ref):
    devices, pieces = recv_ref.shape[0], recv_ref.shape[1] // 3
    groups = devices * pieces
    stencil, nodes = slot_ref.shape[0], slot_ref.shape[1]
    for c in range(3):
        for o in range(devices):
            table_ref[pl.ds(c * groups + o * pieces, pieces), :] = recv_ref[
                o, pl.ds(c * pieces, pieces), :
            ]
    high, low = split_two(table_ref[...])
    both_ref[:, :LANES] = high
    both_ref[:, LANES:] = low
    wide = 2 * LANES
    lane_id = iota((LANES, wide), 0)
    group_id = iota((groups, wide), 0)

    def pair(step, carry):
        sums = [None] * 3
        for t in range(stencil):
            slot = jnp.concatenate(
                [slot_ref[t, pl.ds(2 * step, 1), :], slot_ref[t, pl.ds(2 * step + 1, 1), :]], axis=1
            )
            weight = jnp.concatenate(
                [weight_ref[t, pl.ds(2 * step, 1), :], weight_ref[t, pl.ds(2 * step + 1, 1), :]],
                axis=1,
            )
            pick = (lane_id == slot % LANES).astype(F32).astype(BF16)
            found = jnp.dot(
                both_ref[...], jnp.concatenate([pick, pick], axis=0), preferred_element_type=F32
            )
            scaled = jnp.where(group_id == slot // LANES, weight, 0.0)
            for c in range(3):
                term = found[c * groups : (c + 1) * groups] * scaled
                sums[c] = term if sums[c] is None else sums[c] + term
        for c in range(3):
            line = jnp.sum(sums[c], axis=0, keepdims=True)
            out_ref[c, pl.ds(2 * step, 1), :] = line[:, :LANES]
            out_ref[c, pl.ds(2 * step + 1, 1), :] = line[:, LANES:]
        return carry

    lax.fori_loop(0, nodes // 2, pair, 0)


def swap_corners(corners, flip_y, flip_z):
    middle = {}
    for a, b, c in CORNERS:
        middle[a, b, c] = [
            jnp.where(flip_y, q, p) for p, q in zip(corners[a, b, c], corners[a, 1 - b, c])
        ]
    return {
        (a, b, c): [jnp.where(flip_z, q, p) for p, q in zip(middle[a, b, c], middle[a, b, 1 - c])]
        for a, b, c in CORNERS
    }


def paths():
    for order in STEP_ORDERS:
        position, path = [0, 0, 0], []
        for axis_id in order:
            position[axis_id] = 1
            path.append(tuple(position))
        yield path


def cross(p, q):
    return [p[1] * q[2] - p[2] * q[1], p[2] * q[0] - p[0] * q[2], p[0] * q[1] - p[1] * q[0]]


def add_to(table, key, vector):
    table[key] = [p + q for p, q in zip(table[key], vector)] if key in table else list(vector)


def cell_gradients(offsets, flip_y, flip_z):
    offsets = swap_corners(offsets, flip_y, flip_z)
    sign_y, sign_z = jnp.where(flip_y, -1.0, 1.0), jnp.where(flip_z, -1.0, 1.0)
    anchor = offsets[0, 0, 0]
    edges = {}
    for vertex in CORNERS[1:]:
        edge = [p - q for p, q in zip(offsets[vertex], anchor)]
        if vertex[0]:
            edge[0] = edge[0] + 1.0
        if vertex[1]:
            edge[1] = edge[1] + sign_y
        if vertex[2]:
            edge[2] = edge[2] + sign_z
        edges[vertex] = edge
    gradients, diagonal = [], {}
    for path in paths():
        one, two, three = [edges[v] for v in path]
        across = [cross(two, three), cross(three, one), cross(one, two)]
        volume = one[0] * across[0][0] + one[1] * across[0][1] + one[2] * across[0][2]
        inverse = 1.0 / volume
        grads = [[p * inverse for p in vector] for vector in across]
        gradients.append(grads)
        first = [-(grads[0][p] + grads[1][p] + grads[2][p]) for p in range(3)]
        for vertex, grad in zip([(0, 0, 0)] + path, [first] + grads):
            square = [p * p for p in grad]
            norm = square[0] + square[1] + square[2]
            add_to(diagonal, vertex, [(LAMBDA_RATIO + 1.0) * p + norm for p in square])
    return gradients, swap_corners(diagonal, flip_y, flip_z)


def cell_forces(gradients, motion, flip_y, flip_z):
    motion = swap_corners(motion, flip_y, flip_z)
    anchor = motion[0, 0, 0]
    moves = {v: [p - q for p, q in zip(motion[v], anchor)] for v in CORNERS[1:]}
    forces = {}
    for tet, path in enumerate(paths()):
        grads = [[gradients(tet, v, p) for p in range(3)] for v in range(3)]
        tensor = [
            [
                moves[path[0]][p] * grads[0][q]
                + moves[path[1]][p] * grads[1][q]
                + moves[path[2]][p] * grads[2][q]
                for q in range(3)
            ]
            for p in range(3)
        ]
        trace = LAMBDA_RATIO * (tensor[0][0] + tensor[1][1] + tensor[2][2])
        stress = [[None] * 3 for _ in range(3)]
        for p in range(3):
            stress[p][p] = tensor[p][p] + tensor[p][p] + trace
            for q in range(p):
                stress[p][q] = stress[q][p] = tensor[p][q] + tensor[q][p]
        for v in range(3):
            add_to(
                forces,
                path[v],
                [
                    stress[p][0] * grads[v][0] + stress[p][1] * grads[v][1] + stress[p][2] * grads[v][2]
                    for p in range(3)
                ],
            )
    first = None
    for vector in forces.values():
        first = vector if first is None else [p + q for p, q in zip(first, vector)]
    forces[0, 0, 0] = [-p for p in first]
    return swap_corners(forces, flip_y, flip_z)


def sweep_kernel(field_ref, wall_ref, out_ref, grad_ref, strip_grad_ref, motion_ref, force_ref, diag_ref):
    rows, depth, width = field_ref.shape[1:]
    free = width
    count_y, count_z = out_ref.shape[1:3]
    lane = iota((depth, free), 1)

    def turn(x, shift, axis):
        return pltpu.roll(x, shift % x.shape[axis], axis)

    def main_corners(low, edge):
        corners = {}
        for b in (0, 1):
            for c in (0, 1):
                near = [turn(p, -1, 0) if c else p for p in low[b]]
                corners[0, b, c] = near
                joined = [jnp.where(lane == 0, w, p) for p, w in zip(low[b], edge[b])]
                far = [turn(p, -1, 1) for p in joined]
                corners[1, b, c] = [turn(p, -1, 0) if c else p for p in far]
        return corners

    def main_assemble(parts, b):
        near = [p + turn(q, 1, 0) for p, q in zip(parts[0, b, 0], parts[0, b, 1])]
        far = [p + turn(q, 1, 0) for p, q in zip(parts[1, b, 0], parts[1, b, 1])]
        return [p + jnp.where(lane == 0, 0.0, turn(q, 1, 1)) for p, q in zip(near, far)]

    def strip_corners(near, far):
        corners = {}
        for a, column in ((0, near), (1, far)):
            for b in (0, 1):
                shifted = [turn(p, -1, 1) if b else p for p in column]
                corners[a, b, 0] = shifted
                corners[a, b, 1] = [turn(p, -1, 0) for p in shifted]
        return corners

    def strip_assemble(parts):
        low = [p + turn(q, 1, 0) for p, q in zip(parts[1, 0, 0], parts[1, 0, 1])]
        high = [p + turn(q, 1, 0) for p, q in zip(parts[1, 1, 0], parts[1, 1, 1])]
        return [p + turn(q, 1, 1) for p, q in zip(low, high)]

    def column_strip(read, source):
        total = jnp.zeros((depth, free), F32)
        for j in range(rows):
            total = jnp.where(lane == j, turn(read(j), j - source, 1), total)
        return total

    def codes(value):
        return value >= 1.5, (value == 1.0) | (value == 3.0)

    last = free - 1
    near_offset = [column_strip(lambda j: field_ref[3 + c, j], last) for c in range(3)]
    far_offset = [column_strip(lambda j: field_ref[c, j], 0) for c in range(3)]
    strip_code = column_strip(lambda j: field_ref[7, j], last)
    strip_y, strip_z = codes(strip_code)
    gradients, parts = cell_gradients(strip_corners(near_offset, far_offset), strip_y, strip_z)
    for tet in range(6):
        for v in range(3):
            for p in range(3):
                strip_grad_ref[9 * tet + 3 * v + p] = gradients[tet][v][p]
    strip_diagonal = strip_assemble(parts)
    for j in range(rows):
        for c in range(3):
            diag_ref[j, c] = jnp.where(lane == 0, turn(strip_diagonal[c], -j, 1), 0.0)

    def prepare(j, carry):
        flip_y, flip_z = codes(field_ref[6, j])
        offsets = main_corners(
            [[field_ref[c, j + b] for c in range(3)] for b in (0, 1)],
            [[field_ref[3 + c, j + b] for c in range(3)] for b in (0, 1)],
        )
        gradients, parts = cell_gradients(offsets, flip_y, flip_z)
        for tet in range(6):
            for v in range(3):
                for p in range(3):
                    grad_ref[j, 9 * tet + 3 * v + p] = gradients[tet][v][p]
        for b in (0, 1):
            for c, value in enumerate(main_assemble(parts, b)):
                diag_ref[j + b, c] = diag_ref[j + b, c] + value
        return carry

    lax.fori_loop(0, rows - 1, prepare, 0)
    for c in range(3):
        motion_ref[c] = field_ref[8 + c]
    near_wall = [column_strip(lambda j: wall_ref[c, j], last) for c in range(3)]

    for sweep in range(SWEEPS):
        far_free = [column_strip(lambda j: motion_ref[c, j], 0) for c in range(3)]
        parts = cell_forces(
            lambda tet, v, p: strip_grad_ref[9 * tet + 3 * v + p],
            strip_corners(near_wall, far_free),
            strip_y,
            strip_z,
        )
        strip_force = strip_assemble(parts)
        for j in range(sweep, rows - sweep):
            for c in range(3):
                force_ref[j, c] = jnp.where(lane == 0, turn(strip_force[c], -j, 1), 0.0)

        def push(j, carry):
            flip_y, flip_z = codes(field_ref[6, j])
            motion = main_corners(
                [[motion_ref[c, j + b] for c in range(3)] for b in (0, 1)],
                [[wall_ref[c, j + b] for c in range(3)] for b in (0, 1)],
            )
            parts = cell_forces(
                lambda tet, v, p: grad_ref[j, 9 * tet + 3 * v + p], motion, flip_y, flip_z
            )
            for b in (0, 1):
                for c, value in enumerate(main_assemble(parts, b)):
                    force_ref[j + b, c] = force_ref[j + b, c] + value
            return carry

        lax.fori_loop(sweep, rows - 1 - sweep, push, 0)
        for j in range(sweep + 1, rows - 1 - sweep):
            for c in range(3):
                motion_ref[c, j] = motion_ref[c, j] - RELAX_FACTOR * force_ref[j, c] / diag_ref[j, c]
    for c in range(3):
        for j in range(count_y):
            out_ref[c, j] = motion_ref[c, SWEEPS + j, SWEEPS : SWEEPS + count_z, :]


def call(kernel, out_shape, scratch, *operands):
    spec = pl.BlockSpec(memory_space=pltpu.VMEM)
    return pl.pallas_call(
        kernel,
        out_shape=out_shape,
        in_specs=[spec] * len(operands),
        out_specs=spec,
        scratch_shapes=scratch,
        compiler_params=pltpu.CompilerParams(vmem_limit_bytes=48 << 20),
    )(*operands)


def shards(shell_motion, owner, stencil_slot, stencil_weight, prev_motion, node_offset, cell_split):
    devices = lax.axis_size("struct") * lax.axis_size("fluid")
    own = shell_motion.shape[1]
    capacity = 2 * own // devices
    pieces = capacity // LANES
    slots = devices * capacity
    stencil, count_y, count_z, wall = stencil_slot.shape
    free = prev_motion.shape[3] - wall
    codes = cell_split[None].astype(F32)
    fields = jnp.concatenate(
        [
            node_offset[..., wall:],
            node_offset[..., :wall],
            codes[..., wall:],
            codes[..., :wall],
            prev_motion[..., wall:],
        ],
        axis=0,
    )
    fields = widen(widen(fields, "fluid", 2, SWEEPS), "struct", 1, SWEEPS)
    packed = call(
        functools.partial(pack_kernel, devices, capacity),
        jax.ShapeDtypeStruct((devices, 3 * pieces, LANES), F32),
        [
            pltpu.VMEM((own // LANES, LANES), jnp.int32),
            pltpu.VMEM((3 * slots // (2 * LANES), 2 * LANES), F32),
        ],
        owner.reshape(own // LANES, LANES),
        shell_motion.reshape(3, own // LANES, LANES),
    )
    received = lax.all_to_all(
        packed, ("struct", "fluid"), split_axis=0, concat_axis=0, tiled=True
    )
    wall_values = call(
        wall_kernel,
        jax.ShapeDtypeStruct((3, count_y * count_z, wall), F32),
        [
            pltpu.VMEM((3 * slots // LANES, LANES), F32),
            pltpu.VMEM((3 * slots // LANES, 2 * LANES), BF16),
        ],
        received,
        stencil_slot.reshape(stencil, count_y * count_z, wall),
        stencil_weight.reshape(stencil, count_y * count_z, wall),
    ).reshape(3, count_y, count_z, wall)
    walls = widen(widen(wall_values, "fluid", 2, SWEEPS), "struct", 1, SWEEPS)
    rows, depth = walls.shape[1:3]
    moved = call(
        sweep_kernel,
        jax.ShapeDtypeStruct((3, count_y, count_z, free), F32),
        [
            pltpu.VMEM((rows - 1, 54, depth, free), F32),
            pltpu.VMEM((54, depth, free), F32),
            pltpu.VMEM((3, rows, depth, free), F32),
            pltpu.VMEM((rows, 3, depth, free), F32),
            pltpu.VMEM((rows, 3, depth, free), F32),
        ],
        fields,
        walls,
    )
    return jnp.concatenate([wall_values, moved], axis=3)


def solution(mesh):
    return jax.shard_map(
        shards,
        mesh=mesh,
        in_specs=(
            P(None, ("struct", "fluid")),
            P(("struct", "fluid"), None),
            P(None, "struct", "fluid", None),
            P(None, "struct", "fluid", None),
            P(None, "struct", "fluid", None),
            P(None, "struct", "fluid", None),
            P("struct", "fluid", None),
        ),
        out_specs=P(None, "struct", "fluid", None),
        check_vma=False,
    )
```

time: 183 us -> 67 us (0.37)
  local copies, waits for them, and re-layouts: 74.3 us -> 2.48 us
  waiting for transfers between devices: 61.8 us -> 20 us
  other arithmetic: 27 us -> 0.73 us
  Pallas kernels: 0 us -> 25.3 us
    ppermute x20 -> x10, waiting for transfers between devices: 56.9 us -> 12.8 us  [from_behind(): return lax.ppermute(block, axis, route)]
    gather x1 -> x0, local copies, waits for them, and re-layouts: 31.1 us -> none  [shards(): jnp.take(received, stencil_slot.reshape(-1), axis=1)]
    pallas_call x0 -> x3, Pallas kernels: none -> 25.3 us  [call(): pl.pallas_call(kernel, out_shape=out_shape, in_specs=[spec] * len(operand...]
    scatter x1 -> x0, local copies, waits for them, and re-layouts: 24.5 us -> none  [shards(): jnp.zeros((3, devices * capacity), jnp.float32).at[:, slot_place]]
    another operation x5 -> x0, other arithmetic: 10.1 us -> none
    reduce_sum x49 -> x0, other arithmetic: 8.48 us -> none  [the longest x1 6.13 us: shards(): wall_values = jnp.sum(stencil_weight[None] * gathered, axis=1)]
    reshape x1 -> x0, local copies, waits for them, and re-layouts: 5.95 us -> none  [shards(): packed.reshape(3, devices, capacity)]
    all_to_all x1 -> x0, local copies, waits for them, and re-layouts: 4.83 us -> none  [shards(): lax.all_to_all(packed.reshape(3, devices, capacity), ('struct', 'fluid'),...]
  transfers between devices with their start and end apart: 21 -> 11, of which waited for: 20 -> 8; matrix products, arithmetic and copies ran while one was open for 26% -> 0% of each run, Pallas kernels for 0% -> 19%
where the time goes in v1:
time: 67 us; the launch traced here: 66.7 us
  Pallas kernels  25.3 us (38%)
  waiting for transfers between devices  20 us (30%)
  starting transfers between devices  18 us (27%)
  local copies, waits for them, and re-layouts  2.48 us (4%)
  other arithmetic  0.73 us (1%)
    pallas_call x3, Pallas kernels, call(): pl.pallas_call(kernel, out_shape=out_shape, in_specs=[spec] * len(operand...  25.3 us
    ppermute x10, starting transfers between devices, from_behind(): return lax.ppermute(block, axis, route)  15.4 us
    ppermute x10, waiting for transfers between devices, from_behind(): return lax.ppermute(block, axis, route)  12.8 us
    all_to_all x1, waiting for transfers between devices, shards(): lax.all_to_all(packed, ('struct', 'fluid'), split_axis=0, concat_axis=0,...  7.26 us
    all_to_all x1, starting transfers between devices, shards(): lax.all_to_all(packed, ('struct', 'fluid'), split_axis=0, concat_axis=0,...  2.58 us
    unnamed x25, local copies, waits for them, and re-layouts  2.44 us
  transfers between devices with their start and end apart: 11, of which 8 were waited for; matrix products, arithmetic and copies ran while one was open for 0% of the time, Pallas kernels for 19%

profile of v1, /device:TPU:0, one launch (start us, length us, event | category | flops | bytes accessed | tf_op | source)
XLA Modules:
  0.0 66.7 jit_solution(17637004319161036242)
XLA Ops:
  0.0 0.8 %constant_dynamic-update-slice_fusion.4 = f32[11,2,8,128]{3,2,1,0:T(8,128)S(1)} fusion(f32[3,2,8,256]{3,2,1,0:T(8,128)} %param.12), kind=kLoop, calls=%fused_computation.8 | loop fusion | bytes 49152
  0.8 0.7 %copy-done.5 = s32[2,8,256]{2,1,0:T(8,128)S(1)} copy-done((s32[2,8,256]{2,1,0:T(8,128)S(1)}, s32[2,8,256]{2,1,0:T(8,128)}, u32[]{:S(2)}) %copy-start.5) | copy-done | bytes 16408
  1.7 4.6 %collective-permute-start.1 = (f32[11,2,4,128]{3,2,1,0:T(4,128)S(1)}, f32[11,2,4,128]{3,2,1,0:T(4,128)S(1)}, u32[]{:S(2)}, u32[]{:S(2)}) collective-permute-start(f32[11,2,4,128]{3,2,1,0:T(4,128)S(1)} %get-tuple-element.6), channel_id=1, source_target_pairs={{1,0},{2,1},{3,2},{4,3},{5,4},{6,5},{7,6},{0,7},{9,8},{10,9},{11,1... | collective-permute-start | bytes 135176 | tf_op jit(solution)/shard_map/ppermute | solution.py:23
  6.2 1.7 %collective-permute-done.1 = f32[11,2,4,128]{3,2,1,0:T(4,128)S(1)} collective-permute-done((f32[11,2,4,128]{3,2,1,0:T(4,128)S(1)}, f32[11,2,4,128]{3,2,1,0:T(4,128)S(1)}, u32[]{:S(2)}, u32[]{:S(2)}) %collective-permute-start.1) | collective-permute-done | bytes 45088 | tf_op jit(solution)/shard_map/ppermute | solution.py:23
  7.9 3.6 %collective-permute-done = f32[11,2,4,128]{3,2,1,0:T(4,128)S(1)} collective-permute-done((f32[11,2,4,128]{3,2,1,0:T(4,128)S(1)}, f32[11,2,4,128]{3,2,1,0:T(4,128)S(1)}, u32[]{:S(2)}, u32[]{:S(2)}) %collective-permute-start) | collective-permute-done | bytes 45088 | tf_op jit(solution)/shard_map/ppermute | solution.py:23
  11.5 1.6 %collective-permute-start.2 = (f32[11,2,16,128]{3,2,1,0:T(8,128)S(1)}, f32[11,2,16,128]{3,2,1,0:T(8,128)S(1)}, u32[]{:S(2)}, u32[]{:S(2)}) collective-permute-start(f32[11,2,16,128]{3,2,1,0:T(8,128)S(1)} %pad_maximum_fusion), channel_id=1, source_target_pairs={{16,0},{24,8},{0,16},{8,24},{17,1},{25,9},{1,17},{9,25},{18,2},{26... | collective-permute-start | bytes 540680 | tf_op jit(solution)/shard_map/ppermute | solution.py:23
  13.1 1.5 %collective-permute-start.3 = (f32[11,2,16,128]{3,2,1,0:T(8,128)S(1)}, f32[11,2,16,128]{3,2,1,0:T(8,128)S(1)}, u32[]{:S(2)}, u32[]{:S(2)}) collective-permute-start(f32[11,2,16,128]{3,2,1,0:T(8,128)S(1)} %pad_maximum_fusion), channel_id=1, source_target_pairs={{24,0},{0,8},{8,16},{16,24},{25,1},{1,9},{9,17},{17,25},{26,2},{2,... | collective-permute-start | bytes 540680 | tf_op jit(solution)/shard_map/ppermute | solution.py:23
  14.6 0.7 %copy-done = s32[8192,1]{0,1:T(1,128)S(1)} copy-done((s32[8192,1]{0,1:T(1,128)S(1)}, s32[8192,1]{0,1:T(1,128)}, u32[]{:S(2)}) %copy-start) | copy-done | bytes 32792
  15.4 9.2 %shard_map.73 = f32[32,12,128]{2,1,0:T(8,128)} custom-call(s32[64,128]{1,0:T(8,128)S(1)} %bitcast.15, f32[3,64,128]{2,1,0:T(8,128)S(1)} %bitcast.14), custom_call_target="tpu_custom_call" | custom-call | tf_op jit(solution)/shard_map/pallas_call | solution.py:389
  24.6 2.6 %all-to-all-start = ((f32[32,12,128]{2,1,0:T(8,128)}), f32[32,12,128]{2,1,0:T(8,128)S(1)}, u32[]{:S(2)}, u32[]{:S(2)}) async-start(f32[32,12,128]{2,1,0:T(8,128)} %shard_map.73), calls=%async_computation | async-start | bytes 524288 | tf_op jit(solution)/shard_map/all_to_all | solution.py:429
  27.2 2.6 %collective-permute-start.4 = (f32[11,2,16,128]{3,2,1,0:T(8,128)S(1)}, f32[11,2,16,128]{3,2,1,0:T(8,128)S(1)}, u32[]{:S(2)}, u32[]{:S(2)}) collective-permute-start(f32[11,2,16,128]{3,2,1,0:T(8,128)S(1)} %pad_maximum_fusion), channel_id=1, source_target_pairs={{8,0},{16,8},{24,16},{0,24},{9,1},{17,9},{25,17},{1,25},{10,2},{18... | collective-permute-start | bytes 540680 | tf_op jit(solution)/shard_map/ppermute | solution.py:23
  29.9 7.3 %all-to-all-done.recv_ref = f32[32,12,128]{2,1,0:T(8,128)S(1)} async-done(((f32[32,12,128]{2,1,0:T(8,128)}), f32[32,12,128]{2,1,0:T(8,128)S(1)}, u32[]{:S(2)}, u32[]{:S(2)}) %all-to-all-start) | async-done | bytes 196640 | tf_op jit(solution)/shard_map/all_to_all | solution.py:429
  37.2 3.4 %shard_map.74 = f32[3,16,128]{2,1,0:T(8,128)S(1)} custom-call(f32[32,12,128]{2,1,0:T(8,128)S(1)} %all-to-all-done.recv_ref, s32[4,16,128]{2,1,0:T(8,128)S(1)} %bitcast.16, f32[4,16,128]{2,1,0:T(8,128)S(1)} %bitcast.17), custom_call_target="tpu_custom_call" | custom-call | tf_op jit(solution)/shard_map/pallas_call | solution.py:389
  40.6 1.6 %collective-permute-start.6 = (f32[3,2,4,128]{3,2,1,0:T(4,128)S(1)}, f32[3,2,4,128]{3,2,1,0:T(4,128)S(1)}, u32[]{:S(2)}, u32[]{:S(2)}) collective-permute-start(f32[3,2,4,128]{3,2,1,0:T(4,128)S(1)} %get-tuple-element.8), channel_id=1, source_target_pairs={{1,0},{2,1},{3,2},{4,3},{5,4},{6,5},{7,6},{0,7},{9,8},{10,9},{11,1... | collective-permute-start | bytes 36872 | tf_op jit(solution)/shard_map/ppermute | solution.py:23
  42.2 1.4 %collective-permute-done.6 = f32[3,2,4,128]{3,2,1,0:T(4,128)S(1)} collective-permute-done((f32[3,2,4,128]{3,2,1,0:T(4,128)S(1)}, f32[3,2,4,128]{3,2,1,0:T(4,128)S(1)}, u32[]{:S(2)}, u32[]{:S(2)}) %collective-permute-start.6) | collective-permute-done | bytes 12320 | tf_op jit(solution)/shard_map/ppermute | solution.py:23
  43.6 3.5 %collective-permute-done.5 = f32[3,2,4,128]{3,2,1,0:T(4,128)S(1)} collective-permute-done((f32[3,2,4,128]{3,2,1,0:T(4,128)S(1)}, f32[3,2,4,128]{3,2,1,0:T(4,128)S(1)}, u32[]{:S(2)}, u32[]{:S(2)}) %collective-permute-start.5) | collective-permute-done | bytes 12320 | tf_op jit(solution)/shard_map/ppermute | solution.py:23
  47.1 0.6 collective-permute-start.7
  47.7 1.1 %collective-permute-start.8 = (f32[3,2,16,128]{3,2,1,0:T(8,128)S(1)}, f32[3,2,16,128]{3,2,1,0:T(8,128)S(1)}, u32[]{:S(2)}, u32[]{:S(2)}) collective-permute-start(f32[3,2,16,128]{3,2,1,0:T(8,128)S(1)} %pad_maximum_fusion.1), channel_id=1, source_target_pairs={{24,0},{0,8},{8,16},{16,24},{25,1},{1,9},{9,17},{17,25},{26,2},{2,... | collective-permute-start | bytes 147464 | tf_op jit(solution)/shard_map/ppermute | solution.py:23
  48.8 1.8 %collective-permute-start.9 = (f32[3,2,16,128]{3,2,1,0:T(8,128)S(1)}, f32[3,2,16,128]{3,2,1,0:T(8,128)S(1)}, u32[]{:S(2)}, u32[]{:S(2)}) collective-permute-start(f32[3,2,16,128]{3,2,1,0:T(8,128)S(1)} %pad_maximum_fusion.1), channel_id=1, source_target_pairs={{8,0},{16,8},{24,16},{0,24},{9,1},{17,9},{25,17},{1,25},{10,2},{18... | collective-permute-start | bytes 147464 | tf_op jit(solution)/shard_map/ppermute | solution.py:23
  50.7 0.6 collective-permute-done.7
  51.3 1.5 %collective-permute-done.8 = f32[3,2,16,128]{3,2,1,0:T(8,128)S(1)} collective-permute-done((f32[3,2,16,128]{3,2,1,0:T(8,128)S(1)}, f32[3,2,16,128]{3,2,1,0:T(8,128)S(1)}, u32[]{:S(2)}, u32[]{:S(2)}) %collective-permute-start.8) | collective-permute-done | bytes 49184 | tf_op jit(solution)/shard_map/ppermute | solution.py:23
  52.8 0.6 collective-permute-done.9
  53.4 12.7 %shard_map.75 = f32[3,2,8,128]{3,2,1,0:T(8,128)S(1)} custom-call(f32[11,10,16,128]{3,2,1,0:T(8,128)S(1)} %constant_dynamic-update-slice_fusion.5.field_ref, f32[3,10,16,128]{3,2,1,0:T(8,128)S(1)} %constant_dynamic-update-slice_fusion.10.wall_ref), custom_call_target="tpu_custom_call" | custom-call | tf_op jit(solution)/shard_map/pallas_call | solution.py:389
  66.0 0.6 pad_maximum_fusion.2
  (37 shorter events, 0.3 us)
Async XLA Ops:
  0.0 0.8 %copy-start.4 = (f32[3,2,8,256]{3,2,1,0:T(8,128)S(1)}, f32[3,2,8,256]{3,2,1,0:T(8,128)}, u32[]{:S(2)}) copy-start(f32[3,2,8,256]{3,2,1,0:T(8,128)} %param.12) | copy-start | bytes 147460
  0.8 0.7 %copy-start.5 = (s32[2,8,256]{2,1,0:T(8,128)S(1)}, s32[2,8,256]{2,1,0:T(8,128)}, u32[]{:S(2)}) copy-start(s32[2,8,256]{2,1,0:T(8,128)} %param.13) | copy-start | bytes 49156
  0.8 0.8 %copy-start.6 = (f32[3,2,8,256]{3,2,1,0:T(8,128)S(1)}, f32[3,2,8,256]{3,2,1,0:T(8,128)}, u32[]{:S(2)}) copy-start(f32[3,2,8,256]{3,2,1,0:T(8,128)} %param.11) | copy-start | bytes 147460
  1.7 6.3 %collective-permute-start.1 = (f32[11,2,4,128]{3,2,1,0:T(4,128)S(1)}, f32[11,2,4,128]{3,2,1,0:T(4,128)S(1)}, u32[]{:S(2)}, u32[]{:S(2)}) collective-permute-start(f32[11,2,4,128]{3,2,1,0:T(4,128)S(1)} %get-tuple-element.6), channel_id=1, source_target_pairs={{1,0},{2,1},{3,2},{4,3},{5,4},{6,5},{7,6},{0,7},{9,8},{10,9},{11,1... | collective-permute-start | bytes 135176 | tf_op jit(solution)/shard_map/ppermute | solution.py:23
  6.2 8.4 %copy-start.3 = (f32[3,8192]{1,0:T(4,128)S(1)}, f32[3,8192]{1,0:T(4,128)}, u32[]{:S(2)}) copy-start(f32[3,8192]{1,0:T(4,128)} %param.7) | copy-start | bytes 294916
  6.2 5.3 %collective-permute-start = (f32[11,2,4,128]{3,2,1,0:T(4,128)S(1)}, f32[11,2,4,128]{3,2,1,0:T(4,128)S(1)}, u32[]{:S(2)}, u32[]{:S(2)}) collective-permute-start(f32[11,2,4,128]{3,2,1,0:T(4,128)S(1)} %get-tuple-element.5), channel_id=1, source_target_pairs={{7,0},{0,1},{1,2},{2,3},{3,4},{4,5},{5,6},{6,7},{15,8},{8,9},{9,10... | collective-permute-start | bytes 135176 | tf_op jit(solution)/shard_map/ppermute | solution.py:23
  11.5 18.3 %collective-permute-start.2 = (f32[11,2,16,128]{3,2,1,0:T(8,128)S(1)}, f32[11,2,16,128]{3,2,1,0:T(8,128)S(1)}, u32[]{:S(2)}, u32[]{:S(2)}) collective-permute-start(f32[11,2,16,128]{3,2,1,0:T(8,128)S(1)} %pad_maximum_fusion), channel_id=1, source_target_pairs={{16,0},{24,8},{0,16},{8,24},{17,1},{25,9},{1,17},{9,25},{18,2},{26... | collective-permute-start | bytes 540680 | tf_op jit(solution)/shard_map/ppermute | solution.py:23
  13.1 16.7 %collective-permute-start.3 = (f32[11,2,16,128]{3,2,1,0:T(8,128)S(1)}, f32[11,2,16,128]{3,2,1,0:T(8,128)S(1)}, u32[]{:S(2)}, u32[]{:S(2)}) collective-permute-start(f32[11,2,16,128]{3,2,1,0:T(8,128)S(1)} %pad_maximum_fusion), channel_id=1, source_target_pairs={{24,0},{0,8},{8,16},{16,24},{25,1},{1,9},{9,17},{17,25},{26,2},{2,... | collective-permute-start | bytes 540680 | tf_op jit(solution)/shard_map/ppermute | solution.py:23
  14.6 0.8 %copy-start = (s32[8192,1]{0,1:T(1,128)S(1)}, s32[8192,1]{0,1:T(1,128)}, u32[]{:S(2)}) copy-start(s32[8192,1]{0,1:T(1,128)} %param.8) | copy-start | bytes 98308
  24.6 12.6 %all-to-all-start = ((f32[32,12,128]{2,1,0:T(8,128)}), f32[32,12,128]{2,1,0:T(8,128)S(1)}, u32[]{:S(2)}, u32[]{:S(2)}) async-start(f32[32,12,128]{2,1,0:T(8,128)} %shard_map.73), calls=%async_computation | async-start | bytes 524288 | tf_op jit(solution)/shard_map/all_to_all | solution.py:429
  27.2 15.0 %collective-permute-start.4 = (f32[11,2,16,128]{3,2,1,0:T(8,128)S(1)}, f32[11,2,16,128]{3,2,1,0:T(8,128)S(1)}, u32[]{:S(2)}, u32[]{:S(2)}) collective-permute-start(f32[11,2,16,128]{3,2,1,0:T(8,128)S(1)} %pad_maximum_fusion), channel_id=1, source_target_pairs={{8,0},{16,8},{24,16},{0,24},{9,1},{17,9},{25,17},{1,25},{10,2},{18... | collective-permute-start | bytes 540680 | tf_op jit(solution)/shard_map/ppermute | solution.py:23
  29.8 7.3 %copy-start.1 = (s32[4,2,8,128]{3,2,1,0:T(8,128)S(1)}, s32[4,2,8,128]{3,2,1,0:T(8,128)}, u32[]{:S(2)}) copy-start(s32[4,2,8,128]{3,2,1,0:T(8,128)} %param.9) | copy-start | bytes 98308
  29.9 7.3 %copy-start.2 = (f32[4,2,8,128]{3,2,1,0:T(8,128)S(1)}, f32[4,2,8,128]{3,2,1,0:T(8,128)}, u32[]{:S(2)}) copy-start(f32[4,2,8,128]{3,2,1,0:T(8,128)} %param.10) | copy-start | bytes 98308
  40.6 3.0 %collective-permute-start.6 = (f32[3,2,4,128]{3,2,1,0:T(4,128)S(1)}, f32[3,2,4,128]{3,2,1,0:T(4,128)S(1)}, u32[]{:S(2)}, u32[]{:S(2)}) collective-permute-start(f32[3,2,4,128]{3,2,1,0:T(4,128)S(1)} %get-tuple-element.8), channel_id=1, source_target_pairs={{1,0},{2,1},{3,2},{4,3},{5,4},{6,5},{7,6},{0,7},{9,8},{10,9},{11,1... | collective-permute-start | bytes 36872 | tf_op jit(solution)/shard_map/ppermute | solution.py:23
  42.2 4.9 %collective-permute-start.5 = (f32[3,2,4,128]{3,2,1,0:T(4,128)S(1)}, f32[3,2,4,128]{3,2,1,0:T(4,128)S(1)}, u32[]{:S(2)}, u32[]{:S(2)}) collective-permute-start(f32[3,2,4,128]{3,2,1,0:T(4,128)S(1)} %get-tuple-element.7), channel_id=1, source_target_pairs={{7,0},{0,1},{1,2},{2,3},{3,4},{4,5},{5,6},{6,7},{15,8},{8,9},{9,10... | collective-permute-start | bytes 36872 | tf_op jit(solution)/shard_map/ppermute | solution.py:23
  47.1 4.2 %collective-permute-start.7 = (f32[3,2,16,128]{3,2,1,0:T(8,128)S(1)}, f32[3,2,16,128]{3,2,1,0:T(8,128)S(1)}, u32[]{:S(2)}, u32[]{:S(2)}) collective-permute-start(f32[3,2,16,128]{3,2,1,0:T(8,128)S(1)} %pad_maximum_fusion.1), channel_id=1, source_target_pairs={{16,0},{24,8},{0,16},{8,24},{17,1},{25,9},{1,17},{9,25},{18,2},{26... | collective-permute-start | bytes 147464 | tf_op jit(solution)/shard_map/ppermute | solution.py:23
  47.7 5.0 %collective-permute-start.8 = (f32[3,2,16,128]{3,2,1,0:T(8,128)S(1)}, f32[3,2,16,128]{3,2,1,0:T(8,128)S(1)}, u32[]{:S(2)}, u32[]{:S(2)}) collective-permute-start(f32[3,2,16,128]{3,2,1,0:T(8,128)S(1)} %pad_maximum_fusion.1), channel_id=1, source_target_pairs={{24,0},{0,8},{8,16},{16,24},{25,1},{1,9},{9,17},{17,25},{26,2},{2,... | collective-permute-start | bytes 147464 | tf_op jit(solution)/shard_map/ppermute | solution.py:23
  48.8 4.5 %collective-permute-start.9 = (f32[3,2,16,128]{3,2,1,0:T(8,128)S(1)}, f32[3,2,16,128]{3,2,1,0:T(8,128)S(1)}, u32[]{:S(2)}, u32[]{:S(2)}) collective-permute-start(f32[3,2,16,128]{3,2,1,0:T(8,128)S(1)} %pad_maximum_fusion.1), channel_id=1, source_target_pairs={{8,0},{16,8},{24,16},{0,24},{9,1},{17,9},{25,17},{1,25},{10,2},{18... | collective-permute-start | bytes 147464 | tf_op jit(solution)/shard_map/ppermute | solution.py:23
